TPU v7x, 512 devices: a whole 4x8x8 slice. The times are simulated.
512 devices in a mesh: tm: 4 (over y_hi, core), pix: 128 (over x, z, y_lo).
Axes of the slice: x: 4, y: 8 (y_hi: 2, y_lo: 4; y = y_hi * 4 + y_lo), z: 8, core: 2. Of those that a mesh axis runs over, the one named last changes fastest.
Arguments:
- activations: bfloat16 [4, 327680, 256], P('tm', 'pix'), may hold values from -6 to 6
- down_weight: bfloat16 [1024, 256], replicated, may hold values from -0.1875 to 0.1875
- down_bias: float32 [256], replicated, may hold values from -3 to 3
- taps: float32 [9, 256], replicated, may hold values from -2 to 2
- point_weight: bfloat16 [256, 256], replicated, may hold values from -0.375 to 0.375
- time_mix: float32 [4, 4, 256], replicated, may hold values from -3 to 3
- edge_rows: int32 [128, 2, 20], P('pix'), may hold values from 0 to 19, as said below
- cotangent: bfloat16 [4, 81920, 256], P(None, ('pix', 'tm')), may hold values from -6 to 6
Outputs:
- grad_input: bfloat16 [4, 327680, 256], P('tm', 'pix')
- grad_down: float32 [1024, 256], replicated
- grad_bias: float32 [256], replicated
- grad_taps: float32 [9, 256], replicated
- grad_point: float32 [256, 256], replicated
- grad_mix: float32 [4, 4, 256], replicated
Inputs may be any that keep to these rules, and one draw needn't show every extreme that they name: Each edge_rows[t, e] is either 0, 1, .., 19 or its reversal; edge_rows[t, 1] equals edge_rows[(t + 1) mod 128, 0].
All inputs are finite; a program needn't handle non-finite values.
Results may differ from a plain program's by a relative error of at most 0.014.
Values may be sent and summed in bfloat16 or wider, within the bound.
No kernel may reach another device: no remote copies, remote signals or barrier semaphores. Data moves between devices by JAX's collectives and lax.ppermute only.
A program may use at most 64 MiB of HBM per device.

v0:
```python
import math
import jax
import jax.numpy as jnp
from jax import lax
from jax.sharding import Mesh, PartitionSpec as P

C = 256
TR = 20
TC = 32
TM = ("yh", "core")
PIX = ("x", "z", "yl")
RING = ("yh", "yl")
SUM_ROWS = 1306
PAD_ROWS = 1536


def padded_2(cells, sides, width):
    for axis, dim in sides:
        count = lax.axis_size(axis)
        head = lax.slice_in_dim(cells, 0, width, axis=dim)
        tail = lax.slice_in_dim(cells, cells.shape[dim] - width, cells.shape[dim], axis=dim)
        cells = jnp.concatenate(
            [
                lax.ppermute(tail, axis, [(i, (i + 1) % count) for i in range(count)]),
                cells,
                lax.ppermute(head, axis, [((i + 1) % count, i) for i in range(count)]),
            ],
            axis=dim,
        )
    return cells


def scatter_sum(rows, axis):
    count = lax.axis_size(axis)
    low = rows.astype(jnp.bfloat16).reshape(count, rows.shape[0] // count, C)
    got = lax.all_to_all(low, axis, split_axis=0, concat_axis=0, tiled=True)
    return jnp.sum(got.astype(jnp.float32), axis=0)


def copies(rows, axis):
    count = lax.axis_size(axis)
    wide = jnp.broadcast_to(rows[None], (count,) + rows.shape)
    return lax.all_to_all(wide, axis, split_axis=0, concat_axis=0, tiled=True)


def sum_over_devices(parts):
    half = PAD_ROWS // 2
    core = lax.axis_index("core")
    keep = lax.dynamic_slice_in_dim(parts, core * half, half, axis=0)
    send = lax.dynamic_slice_in_dim(parts, (1 - core) * half, half, axis=0)
    got = lax.ppermute(send.astype(jnp.bfloat16), "core", [(0, 1), (1, 0)])
    rows = keep + got.astype(jnp.float32)
    rows = scatter_sum(rows, "x")
    rows = scatter_sum(rows, "z")
    rows = jnp.sum(copies(rows.astype(jnp.bfloat16), RING).astype(jnp.float32), axis=0)
    rows = rows.astype(jnp.bfloat16)
    rows = copies(rows, "z").reshape(-1, C)
    rows = copies(rows, "x").reshape(-1, C)
    rows = lax.all_gather(rows, "core", axis=0, tiled=True)
    return rows.astype(jnp.float32)


def on_device(
    activations, down_weight, down_bias, taps, point_weight, time_mix, edge_rows, cotangent
):
    frames = lax.axis_size(TM)
    tiles = lax.axis_size(PIX)
    pixels = TR * TC
    scale = 1.0 / math.sqrt(frames * tiles * pixels)
    rows_in = activations.reshape(pixels, 4 * C)
    preact = jnp.dot(rows_in, down_weight, preferred_element_type=jnp.float32) + down_bias
    pooled = jax.nn.silu(preact).astype(jnp.bfloat16)
    tile_grid = pooled.reshape(1, TR, TC, C)
    padded = padded_2(tile_grid, ((PIX, 2),), 1)
    west_map = edge_rows[0, 0]
    east_map = edge_rows[0, 1]
    west_col = jnp.take(padded[0, :, 0, :], west_map, axis=0)
    east_col = jnp.take(padded[0, :, TC + 1, :], east_map, axis=0)
    widened = jnp.concatenate([west_col[:, None, :], tile_grid[0], east_col[:, None, :]], axis=1)
    widened = jnp.pad(widened, ((1, 1), (0, 0), (0, 0)))
    spread = jnp.zeros((TR, TC, C), jnp.float32)
    for row_off in range(3):
        for col_off in range(3):
            spread = (
                spread
                + taps[row_off * 3 + col_off]
                * widened[row_off : row_off + TR, col_off : col_off + TC, :]
            )
    spread_low = spread.astype(jnp.bfloat16).reshape(pixels, C)
    mixed_in = (
        pooled.astype(jnp.float32)
        + jnp.dot(spread_low, point_weight, preferred_element_type=jnp.float32)
    ).astype(jnp.bfloat16)
    by_pixel = lax.all_to_all(
        mixed_in.reshape(1, pixels, C), TM, split_axis=1, concat_axis=0, tiled=True
    )
    mix_part = jnp.einsum("gpc,fpc->fgc", by_pixel, cotangent, preferred_element_type=jnp.float32)
    cot_f = cotangent.astype(jnp.float32)
    mixed_acc = jnp.zeros((frames, cotangent.shape[1], C), jnp.float32)
    for source in range(frames):
        mixed_acc = mixed_acc + time_mix[source][:, None, :] * cot_f[source][None, :, :]
    mixed_grad = mixed_acc.astype(jnp.bfloat16)
    back_grad = lax.all_to_all(mixed_grad, TM, split_axis=0, concat_axis=1, tiled=True)
    mixed_rows = back_grad.reshape(pixels, C)
    point_part = jnp.dot(spread_low.T, mixed_rows, preferred_element_type=jnp.float32)
    spread_grad = jnp.dot(mixed_rows, point_weight.T, preferred_element_type=jnp.float32).astype(
        jnp.bfloat16
    )
    grad_float = spread_grad.reshape(TR, TC, C).astype(jnp.float32)
    taps_rows = []
    for row_off in range(3):
        for col_off in range(3):
            taps_rows.append(
                jnp.sum(
                    grad_float * widened[row_off : row_off + TR, col_off : col_off + TC, :],
                    axis=(0, 1),
                )
            )
    taps_part = jnp.stack(taps_rows, axis=0)
    grad_padded = jnp.pad(grad_float, ((2, 2), (2, 2), (0, 0)))
    wide_grad = jnp.zeros((TR + 2, TC + 2, C), jnp.float32)
    for row_off in range(3):
        for col_off in range(3):
            wide_grad = (
                wide_grad
                + taps[row_off * 3 + col_off]
                * grad_padded[2 - row_off : 4 - row_off + TR, 2 - col_off : 4 - col_off + TC, :]
            )
    west_back = jnp.take(wide_grad[1 : TR + 1, 0, :], west_map, axis=0)
    east_back = jnp.take(wide_grad[1 : TR + 1, TC + 1, :], east_map, axis=0)
    outgoing = jnp.stack([west_back, east_back], axis=1)
    incoming = padded_2(outgoing.astype(jnp.bfloat16), ((PIX, 1),), 1).astype(outgoing.dtype)
    inner_grad = wide_grad[1 : TR + 1, 1 : TC + 1, :]
    inner_grad = inner_grad.at[:, 0, :].add(incoming[:, 0, :])
    inner_grad = inner_grad.at[:, TC - 1, :].add(incoming[:, 3, :])
    pooled_grad = mixed_rows.astype(jnp.float32) + inner_grad.reshape(pixels, C)
    sigma = jax.nn.sigmoid(preact)
    pre_grad = (pooled_grad * (sigma * (1.0 + preact * (1.0 - sigma)))).astype(jnp.bfloat16)
    bias_part = jnp.sum(pre_grad.astype(jnp.float32), axis=0)
    down_part = jnp.dot(rows_in.T, pre_grad, preferred_element_type=jnp.float32)
    grad_input = jnp.dot(pre_grad, down_weight.T, preferred_element_type=jnp.float32).astype(
        jnp.bfloat16
    )
    parts = jnp.concatenate(
        [
            down_part,
            point_part,
            mix_part.reshape(frames * frames, C),
            taps_part,
            bias_part.reshape(1, C),
            jnp.zeros((PAD_ROWS - SUM_ROWS, C), jnp.float32),
        ],
        axis=0,
    )
    total = sum_over_devices(parts) * scale
    grad_down = total[:1024]
    grad_point = total[1024:1280]
    grad_mix = total[1280:1296].reshape(frames, frames, C)
    grad_taps = total[1296:1305]
    grad_bias = total[1305]
    return (
        grad_input.reshape(1, 4 * pixels, C),
        grad_down,
        grad_bias,
        grad_taps,
        grad_point,
        grad_mix,
    )


def solution(mesh):
    chips = Mesh(mesh.devices.reshape(2, 2, 4, 8, 4), ("yh", "core", "x", "z", "yl"))
    in_specs = (
        P(TM, PIX, None),
        P(),
        P(),
        P(),
        P(),
        P(),
        P(PIX, None, None),
        P(None, PIX + TM, None),
    )
    out_specs = (P(TM, PIX, None), P(), P(), P(), P(), P())
    return jax.shard_map(
        on_device, mesh=chips, in_specs=in_specs, out_specs=out_specs, check_vma=False
    )
```

profile of v0, /device:TPU:1, one launch (start us, length us, event | category | flops | bytes accessed | tf_op | source)
XLA Modules:
  0.0 167.9 jit_solution(9329589787763400051)
XLA Ops:
  3.5 10.3 %all-to-all-start = ((bf16[4,160,256]{2,1,0:T(8,128)(2,1)}), bf16[4,160,256]{2,1,0:T(8,128)(2,1)S(1)}, u32[]{:S(2)}, u32[]{:S(2)}) async-start(bf16[4,160,256]{2,1,0:T(8,128)(2,1)} %add_convert_fusion.1), calls=%async_computation | async-start | bytes 655360 | tf_op jit(solution)/shard_map/all_to_all | solution.py:103
  13.8 9.8 %all-to-all-done = bf16[4,160,256]{2,1,0:T(8,128)(2,1)S(1)} async-done(((bf16[4,160,256]{2,1,0:T(8,128)(2,1)}), bf16[4,160,256]{2,1,0:T(8,128)(2,1)S(1)}, u32[]{:S(2)}, u32[]{:S(2)}) %all-to-all-start) | async-done | bytes 327712 | tf_op jit(solution)/shard_map/all_to_all | solution.py:103
  26.5 11.3 %collective-permute-start.1 = (bf16[20,1,256]{2,0,1:T(8,128)(2,1)S(1)}, bf16[20,1,256]{2,0,1:T(8,128)(2,1)S(1)}, u32[]{:S(2)}, u32[]{:S(2)}) collective-permute-start(bf16[20,1,256]{2,0,1:T(8,128)(2,1)S(1)} %fusion.49), channel_id=1, source_target_pairs={{1,0},{2,1},{3,2},{4,3},{5,4},{6,5},{7,6},{8,7},{9,8},{10,9},{11,1... | collective-permute-start | bytes 30728 | tf_op jit(solution)/shard_map/ppermute | solution.py:26
  38.5 1.9 %collective-permute-start = (bf16[20,1,256]{2,0,1:T(8,128)(2,1)S(1)}, bf16[20,1,256]{2,0,1:T(8,128)(2,1)S(1)}, u32[]{:S(2)}, u32[]{:S(2)}) collective-permute-start(bf16[20,1,256]{2,0,1:T(8,128)(2,1)S(1)} %fusion.48), channel_id=1, source_target_pairs={{0,1},{1,2},{2,3},{3,4},{4,5},{5,6},{6,7},{7,8},{8,9},{9,10},{10,1... | collective-permute-start | bytes 30728 | tf_op jit(solution)/shard_map/ppermute | solution.py:24
  41.5 2.5 %reshape.148 = bf16[640,1024]{1,0:T(8,128)(2,1)S(1)} reshape(bf16[1,2560,256]{2,1,0:T(8,128)(2,1)} %param.16) | data formatting | bytes 2621440 | tf_op jit(solution)/shard_map/reshape | solution.py:70
  45.3 3.7 %collective-permute-done = bf16[20,1,256]{2,0,1:T(8,128)(2,1)S(1)} collective-permute-done((bf16[20,1,256]{2,0,1:T(8,128)(2,1)S(1)}, bf16[20,1,256]{2,0,1:T(8,128)(2,1)S(1)}, u32[]{:S(2)}, u32[]{:S(2)}) %collective-permute-start) | collective-permute-done | bytes 10272 | tf_op jit(solution)/shard_map/ppermute | solution.py:24
  50.8 5.7 %collective-permute-start.3 = (bf16[1,20,1,256]{3,1,2,0:T(8,128)(2,1)S(1)}, bf16[1,20,1,256]{3,1,2,0:T(8,128)(2,1)S(1)}, u32[]{:S(2)}, u32[]{:S(2)}) collective-permute-start(bf16[1,20,1,256]{3,1,2,0:T(8,128)(2,1)S(1)} %copy.128), channel_id=1, source_target_pairs={{1,0},{2,1},{3,2},{4,3},{5,4},{6,5},{7,6},{8,7},{9,8},{10,9},{11,1... | collective-permute-start | bytes 30728 | tf_op jit(solution)/shard_map/ppermute | solution.py:26
  56.5 1.9 %collective-permute-start.2 = (bf16[1,20,1,256]{3,1,2,0:T(8,128)(2,1)S(1)}, bf16[1,20,1,256]{3,1,2,0:T(8,128)(2,1)S(1)}, u32[]{:S(2)}, u32[]{:S(2)}) collective-permute-start(bf16[1,20,1,256]{3,1,2,0:T(8,128)(2,1)S(1)} %copy.127), channel_id=1, source_target_pairs={{0,1},{1,2},{2,3},{3,4},{4,5},{5,6},{6,7},{7,8},{8,9},{9,10},{10,1... | collective-permute-start | bytes 30728 | tf_op jit(solution)/shard_map/ppermute | solution.py:24
  58.4 1.6 convolution_bitcast_fusion
  62.2 4.8 %collective-permute-done.2 = bf16[1,20,1,256]{3,1,2,0:T(8,128)(2,1)S(1)} collective-permute-done((bf16[1,20,1,256]{3,1,2,0:T(8,128)(2,1)S(1)}, bf16[1,20,1,256]{3,1,2,0:T(8,128)(2,1)S(1)}, u32[]{:S(2)}, u32[]{:S(2)}) %collective-permute-start.2) | collective-permute-done | bytes 10272 | tf_op jit(solution)/shard_map/ppermute | solution.py:24
  70.0 3.4 %reduce.8 = bf16[640,256]{1,0:T(8,128)(2,1)} reduce(bf16[640,1,256]{2,1,0:T(2,128)(2,1)S(1)} %bitcast.109, bf16[]{:T(256)} %broadcast.133), dimensions={1}, to_apply=%bitcast.98.reduce_sub_computation | reduce | bytes 655362
  73.4 1.8 %reshape.204 = bf16[4,2,20480]{2,1,0:T(2,128)(2,1)} reshape(bf16[640,256]{1,0:T(8,128)(2,1)} %reduce.8) | data formatting | bytes 655360
  75.1 6.4 %all-to-all-start.1 = ((bf16[4,2,20480]{2,1,0:T(2,128)(2,1)}), bf16[4,2,20480]{2,1,0:T(2,128)(2,1)S(1)}, u32[]{:S(2)}, u32[]{:S(2)}) async-start(bf16[4,2,20480]{2,1,0:T(2,128)(2,1)} %reshape.204), calls=%async_computation.1 | async-start | bytes 655360 | tf_op jit(solution)/shard_map/all_to_all | solution.py:94
  89.6 1.7 %all-to-all-done.1 = bf16[4,2,20480]{2,1,0:T(2,128)(2,1)S(1)} async-done(((bf16[4,2,20480]{2,1,0:T(2,128)(2,1)}), bf16[4,2,20480]{2,1,0:T(2,128)(2,1)S(1)}, u32[]{:S(2)}, u32[]{:S(2)}) %all-to-all-start.1) | async-done | bytes 327712 | tf_op jit(solution)/shard_map/all_to_all | solution.py:94
  96.0 3.0 %concatenate.24 = f32[1536,256]{0,1:T(8,128)S(1)} concatenate(f32[1024,256]{0,1:T(8,128)S(1)} %copy-done.1, f32[256,256]{0,1:T(8,128)S(1)} %copy-done.6, f32[16,256]{0,1:T(8,128)} %copy.113, f32[1,256]{0,1:T(8,128)} %copy.114, f32[1,256]{0,1:T(8,128)} %copy.115, f32[1,256]{0,1:T(8,128)} %copy.116, f32[1,256]{0,1:T(8,128)} %copy.117, f32[1,256]{0,1:T(8,128)} %copy.118, ...), dimensions={0} | concatenate | bytes 3145728 | tf_op jit(solution)/shard_map/concatenate | solution.py:144
  99.1 2.8 %collective-permute-start.4 = (bf16[768,256]{0,1:T(8,128)(2,1)S(1)}, bf16[768,256]{0,1:T(8,128)(2,1)S(1)}, u32[]{:S(2)}, u32[]{:S(2)}) collective-permute-start(bf16[768,256]{0,1:T(8,128)(2,1)S(1)} %dynamic-slice_convert_fusion), channel_id=1, source_target_pairs={{0,128},{128,0},{1,129},{129,1},{2,130},{130,2},{3,131},{131,3},{4... | collective-permute-start | bytes 1179656 | tf_op jit(solution)/shard_map/ppermute | solution.py:51
  103.5 10.2 %all_to_all.46 = bf16[4,192,256]{2,1,0:T(8,128)(2,1)S(1)} all-to-all(bf16[4,192,256]{2,1,0:T(8,128)(2,1)S(1)} %bitcast.111), channel_id=1, replica_groups=mesh['yh'=2,'core'=2,'x'=4,'z'=8,'yl'=4] {'x'}, dimensions={0} | all-to-all | bytes 786432 | tf_op jit(solution)/shard_map/all_to_all | solution.py:36
  113.8 10.2 %all_to_all.47 = bf16[8,24,256]{2,1,0:T(8,128)(2,1)S(1)} all-to-all(bf16[8,24,256]{2,1,0:T(8,128)(2,1)S(1)} %bitcast.116), channel_id=1, replica_groups=mesh['yh'=2,'core'=2,'x'=4,'z'=8,'yl'=4] {'z'}, dimensions={0} | all-to-all | bytes 196608 | tf_op jit(solution)/shard_map/all_to_all | solution.py:36
  124.0 11.8 %all_to_all.48 = bf16[8,24,256]{2,1,0:T(8,128)(2,1)S(1)} all-to-all(bf16[8,24,256]{2,1,0:T(8,128)(2,1)S(1)} %broadcast_in_dim.50), channel_id=1, replica_groups=mesh['yh'=2,'core'=2,'x'=4,'z'=8,'yl'=4] {'yh','yl'}, dimensions={0} | all-to-all | bytes 196608 | tf_op jit(solution)/shard_map/all_to_all | solution.py:43
  135.8 10.0 %all_to_all.49 = bf16[8,24,256]{2,1,0:T(8,128)(2,1)S(1)} all-to-all(bf16[8,24,256]{2,1,0:T(8,128)(2,1)S(1)} %broadcast_in_dim.51), channel_id=1, replica_groups=mesh['yh'=2,'core'=2,'x'=4,'z'=8,'yl'=4] {'z'}, dimensions={0} | all-to-all | bytes 196608 | tf_op jit(solution)/shard_map/all_to_all | solution.py:43
  146.6 3.5 %all-to-all-start.6 = ((bf16[4,192,256]{2,1,0:T(8,128)(2,1)}), bf16[4,192,256]{2,1,0:T(8,128)(2,1)S(1)}, u32[]{:S(2)}, u32[]{:S(2)}) async-start(bf16[4,192,256]{2,1,0:T(8,128)(2,1)} %broadcast_in_dim.53), calls=%async_computation.6 | async-start | bytes 786432 | tf_op jit(solution)/shard_map/all_to_all | solution.py:43
  150.6 1.6 reshape.149
  152.2 4.0 %all-to-all-done.6 = bf16[4,192,256]{2,1,0:T(8,128)(2,1)S(1)} async-done(((bf16[4,192,256]{2,1,0:T(8,128)(2,1)}), bf16[4,192,256]{2,1,0:T(8,128)(2,1)S(1)}, u32[]{:S(2)}, u32[]{:S(2)}) %all-to-all-start.6) | async-done | bytes 393248 | tf_op jit(solution)/shard_map/all_to_all | solution.py:43
  156.2 8.0 %all_gather.3 = bf16[1536,256]{1,0:T(8,128)(2,1)S(1)} all-gather(bf16[768,256]{1,0:T(8,128)(2,1)S(1)} %bitcast.112), channel_id=1, replica_groups=mesh['yh'=2,'core'=2,'x'=4,'z'=8,'yl'=4] {'core'}, dimensions={0}, use_global_device_ids=true | all-gather | bytes 1179648 | tf_op jit(solution)/shard_map/all_gather | solution.py:59
  (99 shorter events, 35.0 us)
Async XLA Ops:
  0.6 49.3 %copy-start = (bf16[1024,256]{1,0:T(8,128)(2,1)S(1)}, bf16[1024,256]{1,0:T(8,128)(2,1)}, u32[]{:S(2)}) copy-start(bf16[1024,256]{1,0:T(8,128)(2,1)} %param.17) | copy-start | bytes 1572868
  2.5 11.3 %copy-start.10 = (s32[1,2,20]{2,1,0:T(2,128)S(1)}, s32[1,2,20]{2,1,0:T(2,128)}, u32[]{:S(2)}) copy-start(s32[1,2,20]{2,1,0:T(2,128)} %param.22) | copy-start | bytes 484
  2.5 11.3 %copy-start.9 = (f32[9,256]{1,0:T(8,128)S(1)}, f32[9,256]{1,0:T(8,128)}, u32[]{:S(2)}) copy-start(f32[9,256]{1,0:T(8,128)} %param.19) | copy-start | bytes 27652
  2.5 21.2 %copy-start.7 = (bf16[256,256]{1,0:T(8,128)(2,1)S(1)}, bf16[256,256]{1,0:T(8,128)(2,1)}, u32[]{:S(2)}) copy-start(bf16[256,256]{1,0:T(8,128)(2,1)} %param.20) | copy-start | bytes 393220
  3.5 20.2 %all-to-all-start = ((bf16[4,160,256]{2,1,0:T(8,128)(2,1)}), bf16[4,160,256]{2,1,0:T(8,128)(2,1)S(1)}, u32[]{:S(2)}, u32[]{:S(2)}) async-start(bf16[4,160,256]{2,1,0:T(8,128)(2,1)} %add_convert_fusion.1), calls=%async_computation | async-start | bytes 655360 | tf_op jit(solution)/shard_map/all_to_all | solution.py:103
  24.3 16.1 %copy-start.3 = (bf16[4,160,256]{2,1,0:T(8,128)(2,1)S(1)}, bf16[4,160,256]{2,1,0:T(8,128)(2,1)}, u32[]{:S(2)}) copy-start(bf16[4,160,256]{2,1,0:T(8,128)(2,1)} %param.23) | copy-start | bytes 983044
  24.9 0.9 copy-start.2
  26.5 18.7 %collective-permute-start.1 = (bf16[20,1,256]{2,0,1:T(8,128)(2,1)S(1)}, bf16[20,1,256]{2,0,1:T(8,128)(2,1)S(1)}, u32[]{:S(2)}, u32[]{:S(2)}) collective-permute-start(bf16[20,1,256]{2,0,1:T(8,128)(2,1)S(1)} %fusion.49), channel_id=1, source_target_pairs={{1,0},{2,1},{3,2},{4,3},{5,4},{6,5},{7,6},{8,7},{9,8},{10,9},{11,1... | collective-permute-start | bytes 30728 | tf_op jit(solution)/shard_map/ppermute | solution.py:26
  38.5 10.4 %collective-permute-start = (bf16[20,1,256]{2,0,1:T(8,128)(2,1)S(1)}, bf16[20,1,256]{2,0,1:T(8,128)(2,1)S(1)}, u32[]{:S(2)}, u32[]{:S(2)}) collective-permute-start(bf16[20,1,256]{2,0,1:T(8,128)(2,1)S(1)} %fusion.48), channel_id=1, source_target_pairs={{0,1},{1,2},{2,3},{3,4},{4,5},{5,6},{6,7},{7,8},{8,9},{9,10},{10,1... | collective-permute-start | bytes 30728 | tf_op jit(solution)/shard_map/ppermute | solution.py:24
  44.0 5.9 %copy-start.11 = (f32[256]{0:T(256)S(1)}, f32[256]{0:T(256)}, u32[]{:S(2)}) copy-start(f32[256]{0:T(256)} %param.18) | copy-start | bytes 3076
  50.8 9.3 %copy-start.4 = (bf16[640,256]{1,0:T(8,128)(2,1)}, bf16[640,256]{1,0:T(8,128)(2,1)S(1)}, u32[]{:S(2)}) copy-start(bf16[640,256]{1,0:T(8,128)(2,1)S(1)} %get-tuple-element.53) | copy-start | bytes 983044
  50.8 10.8 %collective-permute-start.3 = (bf16[1,20,1,256]{3,1,2,0:T(8,128)(2,1)S(1)}, bf16[1,20,1,256]{3,1,2,0:T(8,128)(2,1)S(1)}, u32[]{:S(2)}, u32[]{:S(2)}) collective-permute-start(bf16[1,20,1,256]{3,1,2,0:T(8,128)(2,1)S(1)} %copy.128), channel_id=1, source_target_pairs={{1,0},{2,1},{3,2},{4,3},{5,4},{6,5},{7,6},{8,7},{9,8},{10,9},{11,1... | collective-permute-start | bytes 30728 | tf_op jit(solution)/shard_map/ppermute | solution.py:26
  56.5 10.5 %collective-permute-start.2 = (bf16[1,20,1,256]{3,1,2,0:T(8,128)(2,1)S(1)}, bf16[1,20,1,256]{3,1,2,0:T(8,128)(2,1)S(1)}, u32[]{:S(2)}, u32[]{:S(2)}) collective-permute-start(bf16[1,20,1,256]{3,1,2,0:T(8,128)(2,1)S(1)} %copy.127), channel_id=1, source_target_pairs={{0,1},{1,2},{2,3},{3,4},{4,5},{5,6},{6,7},{7,8},{8,9},{9,10},{10,1... | collective-permute-start | bytes 30728 | tf_op jit(solution)/shard_map/ppermute | solution.py:24
  75.1 16.2 %all-to-all-start.1 = ((bf16[4,2,20480]{2,1,0:T(2,128)(2,1)}), bf16[4,2,20480]{2,1,0:T(2,128)(2,1)S(1)}, u32[]{:S(2)}, u32[]{:S(2)}) async-start(bf16[4,2,20480]{2,1,0:T(2,128)(2,1)} %reshape.204), calls=%async_computation.1 | async-start | bytes 655360 | tf_op jit(solution)/shard_map/all_to_all | solution.py:94
  89.6 3.1 %copy-start.8 = (bf16[4,160,256]{1,0,2:T(4,128)(2,1)S(1)}, bf16[4,160,256]{1,0,2:T(4,128)(2,1)}, u32[]{:S(2)}) copy-start(bf16[4,160,256]{1,0,2:T(4,128)(2,1)} %copy.110) | copy-start | bytes 983044
  92.8 3.3 %copy-start.1 = (f32[1024,256]{0,1:T(8,128)S(1)}, f32[1024,256]{0,1:T(8,128)}, u32[]{:S(2)}) copy-start(f32[1024,256]{0,1:T(8,128)} %convolution_bitcast_fusion) | copy-start | bytes 3145732
  92.8 3.3 %copy-start.6 = (f32[256,256]{0,1:T(8,128)S(1)}, f32[256,256]{0,1:T(8,128)}, u32[]{:S(2)}) copy-start(f32[256,256]{0,1:T(8,128)} %fusion.53) | copy-start | bytes 786436
  99.1 4.1 %collective-permute-start.4 = (bf16[768,256]{0,1:T(8,128)(2,1)S(1)}, bf16[768,256]{0,1:T(8,128)(2,1)S(1)}, u32[]{:S(2)}, u32[]{:S(2)}) collective-permute-start(bf16[768,256]{0,1:T(8,128)(2,1)S(1)} %dynamic-slice_convert_fusion), channel_id=1, source_target_pairs={{0,128},{128,0},{1,129},{129,1},{2,130},{130,2},{3,131},{131,3},{4... | collective-permute-start | bytes 1179656 | tf_op jit(solution)/shard_map/ppermute | solution.py:51
  113.7 36.3 %copy-start.5 = (bf16[640,256]{1,0:T(8,128)(2,1)S(1)}, bf16[640,256]{1,0:T(8,128)(2,1)}, u32[]{:S(2)}) copy-start(bf16[640,256]{1,0:T(8,128)(2,1)} %copy-done.4) | copy-start | bytes 983044
  146.6 9.7 %all-to-all-start.6 = ((bf16[4,192,256]{2,1,0:T(8,128)(2,1)}), bf16[4,192,256]{2,1,0:T(8,128)(2,1)S(1)}, u32[]{:S(2)}, u32[]{:S(2)}) async-start(bf16[4,192,256]{2,1,0:T(8,128)(2,1)} %broadcast_in_dim.53), calls=%async_computation.6 | async-start | bytes 786432 | tf_op jit(solution)/shard_map/all_to_all | solution.py:43
where the time goes:
time: 169 us; the launch traced here: 168 us
  blocking collectives  50.1 us (30%)
  starting transfers between devices  43.8 us (26%)
  local copies, waits for them, and re-layouts  32.7 us (19%)
  waiting for transfers between devices  25.4 us (15%)
  other arithmetic  8.94 us (5%)
  matrix products  5.94 us (4%)
    all_to_all x2, blocking collectives, copies(): return lax.all_to_all(wide, axis, split_axis=0, concat_axis=0, tiled=True)  21.7 us
    all_to_all x2, blocking collectives, scatter_sum(): got = lax.all_to_all(low, axis, split_axis=0, concat_axis=0, tiled=True)  20.4 us
    ppermute x2, starting transfers between devices, padded_2(): lax.ppermute(head, axis, [((i + 1) % count, i) for i in range(count)])  17 us
    all_to_all x1, starting transfers between devices, on_device(): lax.all_to_all(mixed_grad, TM, split_axis=0, concat_axis=1, tiled=True)  10.3 us
    all_to_all x1, waiting for transfers between devices, on_device(): lax.all_to_all(mixed_grad, TM, split_axis=0, concat_axis=1, tiled=True)  9.85 us
    ppermute x2, waiting for transfers between devices, padded_2(): lax.ppermute(tail, axis, [(i, (i + 1) % count) for i in range(count)])  8.5 us
    all_gather x1, blocking collectives, sum_over_devices(): rows = lax.all_gather(rows, 'core', axis=0, tiled=True)  7.95 us
    another operation x9, local copies, waits for them, and re-layouts, on_device(): taps_part = jnp.stack(taps_rows, axis=0)  7.14 us
  transfers between devices with their start and end apart: 8, of which 6 were waited for; matrix products, arithmetic and copies ran while one was open for 12% of the time, Pallas kernels for 0%

commit v1 on v0

--- a/solution.py
+++ b/solution.py
@@ -56,7 +56,10 @@
     rows = rows.astype(jnp.bfloat16)
     rows = copies(rows, "z").reshape(-1, C)
     rows = copies(rows, "x").reshape(-1, C)
-    rows = lax.all_gather(rows, "core", axis=0, tiled=True)
+    size = lax.axis_size("core")
+    pieces = jnp.stack([rows for _ in range(size)])
+    pieces = lax.all_to_all(pieces, "core", split_axis=0, concat_axis=0)
+    rows = jnp.concatenate(pieces, axis=0)
     return rows.astype(jnp.float32)
 
 

time: 169 us -> 170 us (level)
    all_to_all x0 -> x1, blocking collectives: none -> 9.96 us  [sum_over_devices(): pieces = lax.all_to_all(pieces, 'core', split_axis=0, concat_axis=0)]
    all_gather x1 -> x0, blocking collectives: 7.95 us -> none  [sum_over_devices(): rows = lax.all_gather(rows, 'core', axis=0, tiled=True)]
    unnamed x31 -> x51, local copies, waits for them, and re-layouts: 4.66 us -> 2.86 us
  transfers between devices with their start and end apart: 8 -> 8, of which waited for: 6 -> 6; matrix products, arithmetic and copies ran while one was open for 12% -> 11% of each run, Pallas kernels for 0% -> 0%
where the time goes in v1:
time: 170 us; the launch traced here: 169 us
  blocking collectives  51.5 us (30%)
  starting transfers between devices  43.8 us (26%)
  local copies, waits for them, and re-layouts  31.1 us (18%)
  waiting for transfers between devices  26.6 us (16%)
  other arithmetic  9.19 us (5%)
  matrix products  5.24 us (3%)
    all_to_all x2, blocking collectives, copies(): return lax.all_to_all(wide, axis, split_axis=0, concat_axis=0, tiled=True)  21.2 us
    all_to_all x2, blocking collectives, scatter_sum(): got = lax.all_to_all(low, axis, split_axis=0, concat_axis=0, tiled=True)  20.4 us
    ppermute x2, starting transfers between devices, padded_2(): lax.ppermute(head, axis, [((i + 1) % count, i) for i in range(count)])  17 us
    all_to_all x1, starting transfers between devices, on_device(): lax.all_to_all(mixed_grad, TM, split_axis=0, concat_axis=1, tiled=True)  10.3 us
    all_to_all x1, blocking collectives, sum_over_devices(): pieces = lax.all_to_all(pieces, 'core', split_axis=0, concat_axis=0)  9.96 us
    all_to_all x1, waiting for transfers between devices, on_device(): lax.all_to_all(mixed_grad, TM, split_axis=0, concat_axis=1, tiled=True)  9.81 us
    ppermute x2, waiting for transfers between devices, padded_2(): lax.ppermute(tail, axis, [(i, (i + 1) % count) for i in range(count)])  9.13 us
    another operation x9, local copies, waits for them, and re-layouts, on_device(): taps_part = jnp.stack(taps_rows, axis=0)  7.22 us
  transfers between devices with their start and end apart: 8, of which 6 were waited for; matrix products, arithmetic and copies ran while one was open for 11% of the time, Pallas kernels for 0%

profile of v1, /device:TPU:1, one launch (start us, length us, event | category | flops | bytes accessed | tf_op | source)
XLA Modules:
  0.0 168.6 jit_solution(1267853126942956874)
XLA Ops:
  3.5 10.3 %all-to-all-start = ((bf16[4,160,256]{2,1,0:T(8,128)(2,1)}), bf16[4,160,256]{2,1,0:T(8,128)(2,1)S(1)}, u32[]{:S(2)}, u32[]{:S(2)}) async-start(bf16[4,160,256]{2,1,0:T(8,128)(2,1)} %add_convert_fusion.1), calls=%async_computation | async-start | bytes 655360 | tf_op jit(solution)/shard_map/all_to_all | solution.py:106
  13.9 9.8 %all-to-all-done = bf16[4,160,256]{2,1,0:T(8,128)(2,1)S(1)} async-done(((bf16[4,160,256]{2,1,0:T(8,128)(2,1)}), bf16[4,160,256]{2,1,0:T(8,128)(2,1)S(1)}, u32[]{:S(2)}, u32[]{:S(2)}) %all-to-all-start) | async-done | bytes 327712 | tf_op jit(solution)/shard_map/all_to_all | solution.py:106
  27.3 11.3 %collective-permute-start.1 = (bf16[20,1,256]{2,0,1:T(8,128)(2,1)S(1)}, bf16[20,1,256]{2,0,1:T(8,128)(2,1)S(1)}, u32[]{:S(2)}, u32[]{:S(2)}) collective-permute-start(bf16[20,1,256]{2,0,1:T(8,128)(2,1)S(1)} %fusion.49), channel_id=1, source_target_pairs={{1,0},{2,1},{3,2},{4,3},{5,4},{6,5},{7,6},{8,7},{9,8},{10,9},{11,1... | collective-permute-start | bytes 30728 | tf_op jit(solution)/shard_map/ppermute | solution.py:26
  39.3 1.9 %collective-permute-start = (bf16[20,1,256]{2,0,1:T(8,128)(2,1)S(1)}, bf16[20,1,256]{2,0,1:T(8,128)(2,1)S(1)}, u32[]{:S(2)}, u32[]{:S(2)}) collective-permute-start(bf16[20,1,256]{2,0,1:T(8,128)(2,1)S(1)} %fusion.48), channel_id=1, source_target_pairs={{0,1},{1,2},{2,3},{3,4},{4,5},{5,6},{6,7},{7,8},{8,9},{9,10},{10,1... | collective-permute-start | bytes 30728 | tf_op jit(solution)/shard_map/ppermute | solution.py:24
  42.3 2.5 %reshape.149 = bf16[640,1024]{1,0:T(8,128)(2,1)S(1)} reshape(bf16[1,2560,256]{2,1,0:T(8,128)(2,1)} %param.16) | data formatting | bytes 2621440 | tf_op jit(solution)/shard_map/reshape | solution.py:73
  46.0 3.7 %collective-permute-done = bf16[20,1,256]{2,0,1:T(8,128)(2,1)S(1)} collective-permute-done((bf16[20,1,256]{2,0,1:T(8,128)(2,1)S(1)}, bf16[20,1,256]{2,0,1:T(8,128)(2,1)S(1)}, u32[]{:S(2)}, u32[]{:S(2)}) %collective-permute-start) | collective-permute-done | bytes 10272 | tf_op jit(solution)/shard_map/ppermute | solution.py:24
  51.6 5.7 %collective-permute-start.3 = (bf16[1,20,1,256]{3,1,2,0:T(8,128)(2,1)S(1)}, bf16[1,20,1,256]{3,1,2,0:T(8,128)(2,1)S(1)}, u32[]{:S(2)}, u32[]{:S(2)}) collective-permute-start(bf16[1,20,1,256]{3,1,2,0:T(8,128)(2,1)S(1)} %copy.128), channel_id=1, source_target_pairs={{1,0},{2,1},{3,2},{4,3},{5,4},{6,5},{7,6},{8,7},{9,8},{10,9},{11,1... | collective-permute-start | bytes 30728 | tf_op jit(solution)/shard_map/ppermute | solution.py:26
  57.3 1.9 %collective-permute-start.2 = (bf16[1,20,1,256]{3,1,2,0:T(8,128)(2,1)S(1)}, bf16[1,20,1,256]{3,1,2,0:T(8,128)(2,1)S(1)}, u32[]{:S(2)}, u32[]{:S(2)}) collective-permute-start(bf16[1,20,1,256]{3,1,2,0:T(8,128)(2,1)S(1)} %copy.127), channel_id=1, source_target_pairs={{0,1},{1,2},{2,3},{3,4},{4,5},{5,6},{6,7},{7,8},{8,9},{9,10},{10,1... | collective-permute-start | bytes 30728 | tf_op jit(solution)/shard_map/ppermute | solution.py:24
  59.2 1.6 convolution_bitcast_fusion
  62.4 5.4 %collective-permute-done.2 = bf16[1,20,1,256]{3,1,2,0:T(8,128)(2,1)S(1)} collective-permute-done((bf16[1,20,1,256]{3,1,2,0:T(8,128)(2,1)S(1)}, bf16[1,20,1,256]{3,1,2,0:T(8,128)(2,1)S(1)}, u32[]{:S(2)}, u32[]{:S(2)}) %collective-permute-start.2) | collective-permute-done | bytes 10272 | tf_op jit(solution)/shard_map/ppermute | solution.py:24
  70.9 2.7 %reduce.8 = bf16[640,256]{1,0:T(8,128)(2,1)S(1)} reduce(bf16[640,1,256]{2,1,0:T(2,128)(2,1)S(1)} %bitcast.115, bf16[]{:T(256)} %broadcast.135), dimensions={1}, to_apply=%bitcast.99.reduce_sub_computation | reduce | bytes 655362
  74.4 6.4 %all-to-all-start.1 = ((bf16[4,2,20480]{2,1,0:T(2,128)(2,1)}), bf16[4,2,20480]{2,1,0:T(2,128)(2,1)S(1)}, u32[]{:S(2)}, u32[]{:S(2)}) async-start(bf16[4,2,20480]{2,1,0:T(2,128)(2,1)} %reshape.204), calls=%async_computation.1 | async-start | bytes 655360 | tf_op jit(solution)/shard_map/all_to_all | solution.py:97
  88.2 2.3 %all-to-all-done.1 = bf16[4,2,20480]{2,1,0:T(2,128)(2,1)S(1)} async-done(((bf16[4,2,20480]{2,1,0:T(2,128)(2,1)}), bf16[4,2,20480]{2,1,0:T(2,128)(2,1)S(1)}, u32[]{:S(2)}, u32[]{:S(2)}) %all-to-all-start.1) | async-done | bytes 327712 | tf_op jit(solution)/shard_map/all_to_all | solution.py:97
  92.0 1.5 convolution_bitcast_fusion.1
  95.2 3.0 %concatenate.24 = f32[1536,256]{0,1:T(8,128)S(1)} concatenate(f32[1024,256]{0,1:T(8,128)S(1)} %copy-done.1, f32[256,256]{0,1:T(8,128)S(1)} %fusion.53, f32[16,256]{0,1:T(8,128)} %copy.113, f32[1,256]{0,1:T(8,128)} %copy.114, f32[1,256]{0,1:T(8,128)} %copy.115, f32[1,256]{0,1:T(8,128)} %copy.116, f32[1,256]{0,1:T(8,128)} %copy.117, f32[1,256]{0,1:T(8,128)} %copy.118, ...), dimensions={0} | concatenate | bytes 3145728 | tf_op jit(solution)/shard_map/concatenate | solution.py:147
  98.3 2.8 %collective-permute-start.4 = (bf16[768,256]{0,1:T(8,128)(2,1)S(1)}, bf16[768,256]{0,1:T(8,128)(2,1)S(1)}, u32[]{:S(2)}, u32[]{:S(2)}) collective-permute-start(bf16[768,256]{0,1:T(8,128)(2,1)S(1)} %dynamic-slice_convert_fusion), channel_id=1, source_target_pairs={{0,128},{128,0},{1,129},{129,1},{2,130},{130,2},{3,131},{131,3},{4... | collective-permute-start | bytes 1179656 | tf_op jit(solution)/shard_map/ppermute | solution.py:51
  102.7 10.2 %all_to_all.51 = bf16[4,192,256]{2,1,0:T(8,128)(2,1)S(1)} all-to-all(bf16[4,192,256]{2,1,0:T(8,128)(2,1)S(1)} %bitcast.117), channel_id=1, replica_groups=mesh['yh'=2,'core'=2,'x'=4,'z'=8,'yl'=4] {'x'}, dimensions={0} | all-to-all | bytes 786432 | tf_op jit(solution)/shard_map/all_to_all | solution.py:36
  113.0 10.2 %all_to_all.52 = bf16[8,24,256]{2,1,0:T(8,128)(2,1)S(1)} all-to-all(bf16[8,24,256]{2,1,0:T(8,128)(2,1)S(1)} %bitcast.122), channel_id=1, replica_groups=mesh['yh'=2,'core'=2,'x'=4,'z'=8,'yl'=4] {'z'}, dimensions={0} | all-to-all | bytes 196608 | tf_op jit(solution)/shard_map/all_to_all | solution.py:36
  123.2 11.2 %all_to_all.53 = bf16[8,24,256]{2,1,0:T(8,128)(2,1)S(1)} all-to-all(bf16[8,24,256]{2,1,0:T(8,128)(2,1)S(1)} %broadcast_in_dim.50), channel_id=1, replica_groups=mesh['yh'=2,'core'=2,'x'=4,'z'=8,'yl'=4] {'yh','yl'}, dimensions={0} | all-to-all | bytes 196608 | tf_op jit(solution)/shard_map/all_to_all | solution.py:43
  134.5 10.0 %all_to_all.54 = bf16[8,24,256]{2,1,0:T(8,128)(2,1)S(1)} all-to-all(bf16[8,24,256]{2,1,0:T(8,128)(2,1)S(1)} %broadcast_in_dim.51), channel_id=1, replica_groups=mesh['yh'=2,'core'=2,'x'=4,'z'=8,'yl'=4] {'z'}, dimensions={0} | all-to-all | bytes 196608 | tf_op jit(solution)/shard_map/all_to_all | solution.py:43
  145.2 3.5 %all-to-all-start.6 = ((bf16[4,192,256]{2,1,0:T(8,128)(2,1)}), bf16[4,192,256]{2,1,0:T(8,128)(2,1)S(1)}, u32[]{:S(2)}, u32[]{:S(2)}) async-start(bf16[4,192,256]{2,1,0:T(8,128)(2,1)} %broadcast_in_dim.53), calls=%async_computation.6 | async-start | bytes 786432 | tf_op jit(solution)/shard_map/all_to_all | solution.py:43
  149.2 1.6 reshape.150
  150.9 4.0 %all-to-all-done.6 = bf16[4,192,256]{2,1,0:T(8,128)(2,1)S(1)} async-done(((bf16[4,192,256]{2,1,0:T(8,128)(2,1)}), bf16[4,192,256]{2,1,0:T(8,128)(2,1)S(1)}, u32[]{:S(2)}, u32[]{:S(2)}) %all-to-all-start.6) | async-done | bytes 393248 | tf_op jit(solution)/shard_map/all_to_all | solution.py:43
  154.9 10.0 %all_to_all.55 = bf16[2,768,256]{2,1,0:T(8,128)(2,1)S(1)} all-to-all(bf16[2,768,256]{2,1,0:T(8,128)(2,1)S(1)} %pad_maximum_fusion), channel_id=1, replica_groups=mesh['yh'=2,'core'=2,'x'=4,'z'=8,'yl'=4] {'core'}, dimensions={0} | all-to-all | bytes 1572864 | tf_op jit(solution)/shard_map/all_to_all | solution.py:61
  (120 shorter events, 33.9 us)
Async XLA Ops:
  0.6 50.1 %copy-start = (bf16[1024,256]{1,0:T(8,128)(2,1)S(1)}, bf16[1024,256]{1,0:T(8,128)(2,1)}, u32[]{:S(2)}) copy-start(bf16[1024,256]{1,0:T(8,128)(2,1)} %param.17) | copy-start | bytes 1572868
  2.5 11.3 %copy-start.20 = (s32[1,2,20]{2,1,0:T(2,128)S(1)}, s32[1,2,20]{2,1,0:T(2,128)}, u32[]{:S(2)}) copy-start(s32[1,2,20]{2,1,0:T(2,128)} %param.22) | copy-start | bytes 484
  2.5 11.3 %copy-start.19 = (f32[9,256]{1,0:T(8,128)S(1)}, f32[9,256]{1,0:T(8,128)}, u32[]{:S(2)}) copy-start(f32[9,256]{1,0:T(8,128)} %param.19) | copy-start | bytes 27652
  2.5 21.2 %copy-start.7 = (bf16[256,256]{1,0:T(8,128)(2,1)S(1)}, bf16[256,256]{1,0:T(8,128)(2,1)}, u32[]{:S(2)}) copy-start(bf16[256,256]{1,0:T(8,128)(2,1)} %param.20) | copy-start | bytes 393220
  3.5 20.2 %all-to-all-start = ((bf16[4,160,256]{2,1,0:T(8,128)(2,1)}), bf16[4,160,256]{2,1,0:T(8,128)(2,1)S(1)}, u32[]{:S(2)}, u32[]{:S(2)}) async-start(bf16[4,160,256]{2,1,0:T(8,128)(2,1)} %add_convert_fusion.1), calls=%async_computation | async-start | bytes 655360 | tf_op jit(solution)/shard_map/all_to_all | solution.py:106
  13.8 10.5 %copy-start.13 = (f32[1,256]{1,0:T(1,128)}, f32[1,256]{1,0:T(1,128)S(1)}, u32[]{:S(2)}) copy-start(f32[1,256]{1,0:T(1,128)S(1)} %get-tuple-element.66) | copy-start | bytes 3076
  13.8 10.5 %copy-start.15 = (f32[1,256]{1,0:T(1,128)}, f32[1,256]{1,0:T(1,128)S(1)}, u32[]{:S(2)}) copy-start(f32[1,256]{1,0:T(1,128)S(1)} %get-tuple-element.67) | copy-start | bytes 3076
  13.8 10.5 %copy-start.17 = (f32[1,256]{1,0:T(1,128)}, f32[1,256]{1,0:T(1,128)S(1)}, u32[]{:S(2)}) copy-start(f32[1,256]{1,0:T(1,128)S(1)} %get-tuple-element.68) | copy-start | bytes 3076
  23.7 27.1 %copy-start.2 = (bf16[4,160,256]{2,1,0:T(8,128)(2,1)}, bf16[4,160,256]{2,1,0:T(8,128)(2,1)S(1)}, u32[]{:S(2)}) copy-start(bf16[4,160,256]{2,1,0:T(8,128)(2,1)S(1)} %all-to-all-done) | copy-start | bytes 983044
  24.4 16.9 %copy-start.4 = (bf16[4,160,256]{2,1,0:T(8,128)(2,1)S(1)}, bf16[4,160,256]{2,1,0:T(8,128)(2,1)}, u32[]{:S(2)}) copy-start(bf16[4,160,256]{2,1,0:T(8,128)(2,1)} %param.23) | copy-start | bytes 983044
  27.3 18.7 %collective-permute-start.1 = (bf16[20,1,256]{2,0,1:T(8,128)(2,1)S(1)}, bf16[20,1,256]{2,0,1:T(8,128)(2,1)S(1)}, u32[]{:S(2)}, u32[]{:S(2)}) collective-permute-start(bf16[20,1,256]{2,0,1:T(8,128)(2,1)S(1)} %fusion.49), channel_id=1, source_target_pairs={{1,0},{2,1},{3,2},{4,3},{5,4},{6,5},{7,6},{8,7},{9,8},{10,9},{11,1... | collective-permute-start | bytes 30728 | tf_op jit(solution)/shard_map/ppermute | solution.py:26
  39.3 10.4 %collective-permute-start = (bf16[20,1,256]{2,0,1:T(8,128)(2,1)S(1)}, bf16[20,1,256]{2,0,1:T(8,128)(2,1)S(1)}, u32[]{:S(2)}, u32[]{:S(2)}) collective-permute-start(bf16[20,1,256]{2,0,1:T(8,128)(2,1)S(1)} %fusion.48), channel_id=1, source_target_pairs={{0,1},{1,2},{2,3},{3,4},{4,5},{5,6},{6,7},{7,8},{8,9},{9,10},{10,1... | collective-permute-start | bytes 30728 | tf_op jit(solution)/shard_map/ppermute | solution.py:24
  51.6 9.2 %copy-start.5 = (bf16[640,256]{1,0:T(8,128)(2,1)}, bf16[640,256]{1,0:T(8,128)(2,1)S(1)}, u32[]{:S(2)}) copy-start(bf16[640,256]{1,0:T(8,128)(2,1)S(1)} %get-tuple-element.53) | copy-start | bytes 983044
  51.6 10.1 %collective-permute-start.3 = (bf16[1,20,1,256]{3,1,2,0:T(8,128)(2,1)S(1)}, bf16[1,20,1,256]{3,1,2,0:T(8,128)(2,1)S(1)}, u32[]{:S(2)}, u32[]{:S(2)}) collective-permute-start(bf16[1,20,1,256]{3,1,2,0:T(8,128)(2,1)S(1)} %copy.128), channel_id=1, source_target_pairs={{1,0},{2,1},{3,2},{4,3},{5,4},{6,5},{7,6},{8,7},{9,8},{10,9},{11,1... | collective-permute-start | bytes 30728 | tf_op jit(solution)/shard_map/ppermute | solution.py:26
  57.3 10.5 %collective-permute-start.2 = (bf16[1,20,1,256]{3,1,2,0:T(8,128)(2,1)S(1)}, bf16[1,20,1,256]{3,1,2,0:T(8,128)(2,1)S(1)}, u32[]{:S(2)}, u32[]{:S(2)}) collective-permute-start(bf16[1,20,1,256]{3,1,2,0:T(8,128)(2,1)S(1)} %copy.127), channel_id=1, source_target_pairs={{0,1},{1,2},{2,3},{3,4},{4,5},{5,6},{6,7},{7,8},{8,9},{9,10},{10,1... | collective-permute-start | bytes 30728 | tf_op jit(solution)/shard_map/ppermute | solution.py:24
  60.8 7.9 %copy-start.14 = (f32[1,256]{1,0:T(1,128)S(1)}, f32[1,256]{1,0:T(1,128)}, u32[]{:S(2)}) copy-start(f32[1,256]{1,0:T(1,128)} %copy-done.13) | copy-start | bytes 3076
  60.8 8.0 %copy-start.16 = (f32[1,256]{1,0:T(1,128)S(1)}, f32[1,256]{1,0:T(1,128)}, u32[]{:S(2)}) copy-start(f32[1,256]{1,0:T(1,128)} %copy-done.15) | copy-start | bytes 3076
  60.8 8.0 %copy-start.18 = (f32[1,256]{1,0:T(1,128)S(1)}, f32[1,256]{1,0:T(1,128)}, u32[]{:S(2)}) copy-start(f32[1,256]{1,0:T(1,128)} %copy-done.17) | copy-start | bytes 3076
  70.3 10.4 %copy-start.10 = (bf16[20,1,256]{2,1,0:T(2,128)(2,1)S(1)}, bf16[20,1,256]{2,1,0:T(2,128)(2,1)}, u32[]{:S(2)}) copy-start(bf16[20,1,256]{2,1,0:T(2,128)(2,1)} %copy-done.9) | copy-start | bytes 30724
  70.3 10.4 %copy-start.12 = (bf16[20,1,256]{2,1,0:T(2,128)(2,1)S(1)}, bf16[20,1,256]{2,1,0:T(2,128)(2,1)}, u32[]{:S(2)}) copy-start(bf16[20,1,256]{2,1,0:T(2,128)(2,1)} %copy-done.11) | copy-start | bytes 30724
  74.4 16.2 %all-to-all-start.1 = ((bf16[4,2,20480]{2,1,0:T(2,128)(2,1)}), bf16[4,2,20480]{2,1,0:T(2,128)(2,1)S(1)}, u32[]{:S(2)}, u32[]{:S(2)}) async-start(bf16[4,2,20480]{2,1,0:T(2,128)(2,1)} %reshape.204), calls=%async_computation.1 | async-start | bytes 655360 | tf_op jit(solution)/shard_map/all_to_all | solution.py:97
  98.3 4.1 %collective-permute-start.4 = (bf16[768,256]{0,1:T(8,128)(2,1)S(1)}, bf16[768,256]{0,1:T(8,128)(2,1)S(1)}, u32[]{:S(2)}, u32[]{:S(2)}) collective-permute-start(bf16[768,256]{0,1:T(8,128)(2,1)S(1)} %dynamic-slice_convert_fusion), channel_id=1, source_target_pairs={{0,128},{128,0},{1,129},{129,1},{2,130},{130,2},{3,131},{131,3},{4... | collective-permute-start | bytes 1179656 | tf_op jit(solution)/shard_map/ppermute | solution.py:51
  112.9 35.7 %copy-start.6 = (bf16[640,256]{1,0:T(8,128)(2,1)S(1)}, bf16[640,256]{1,0:T(8,128)(2,1)}, u32[]{:S(2)}) copy-start(bf16[640,256]{1,0:T(8,128)(2,1)} %copy-done.5) | copy-start | bytes 983044
  145.2 9.7 %all-to-all-start.6 = ((bf16[4,192,256]{2,1,0:T(8,128)(2,1)}), bf16[4,192,256]{2,1,0:T(8,128)(2,1)S(1)}, u32[]{:S(2)}, u32[]{:S(2)}) async-start(bf16[4,192,256]{2,1,0:T(8,128)(2,1)} %broadcast_in_dim.53), calls=%async_computation.6 | async-start | bytes 786432 | tf_op jit(solution)/shard_map/all_to_all | solution.py:43
  (6 other events, 22.2 us)
